TPU v7x, 512 devices: a whole 4x4x16 slice. The times are simulated.
512 devices in a mesh: gz: 8 (over y, core), xy: 64 (over x, z).
Axes of the slice: x: 4, y: 4, z: 16, core: 2. Of those that a mesh axis runs over, the one named last changes fastest.
Arguments:
- velocity_free: float32 [8, 64, 6, 512], P('gz', 'xy'), may hold values from -6 to 6
- inverse_mass: float32 [8, 64, 2, 512], P('gz', 'xy'), may hold values from 0.25 to 4
- jacobian: float32 [8, 64, 36, 2048], P('gz', 'xy'), may hold values from -1.75 to 1.75
- impulses: float32 [8, 64, 3, 2048], P('gz', 'xy'), may hold values from -6 to 6
- previous_impulses: float32 [8, 64, 3, 2048], P('gz', 'xy'), may hold values from -6 to 6
- compliance: float32 [8, 64, 2048], P('gz', 'xy'), may hold values from 0.05 to 0.5
- offset: float32 [8, 64, 2048], P('gz', 'xy'), may hold values from -6 to 6
- friction: float32 [8, 64, 2048], P('gz', 'xy'), may hold values from 0.2 to 0.8
- body_near: int32 [8, 64, 2048], P('gz', 'xy'), may hold values from 0 to 511
- body_far: int32 [8, 64, 2048], P('gz', 'xy'), may hold values from 0 to 1023
- block_counts: int32 [8, 64, 16], P('gz', 'xy'), may hold values from 0 to 128, as said below
- layer_send: int32 [8, 64, 128], P('gz', 'xy'), may hold values from 0 to 511
- side_send: int32 [8, 64, 2, 192], P('gz', 'xy'), may hold values from 0 to 639
Outputs:
- impulses_out: float32 [8, 64, 3, 2048], P('gz', 'xy')
- velocity_out: float32 [8, 64, 6, 512], P('gz', 'xy')
Inputs may be any that keep to these rules, and one draw needn't show every extreme that they name: `block_counts`: on each device the blocks that hold live contacts come first, every one of them but the last full; some device holds 2048 live contacts. `body_far`: entries of 512 or more name received rows: 512 + i is the row received as the i-th from the layer above, then 192 rows from the lower-side and 192 from the higher-side neighbour. `side_send`: entries of 512 or more name rows received from the layer above.
All inputs are finite; a program needn't handle non-finite values.
Results may differ from a plain program's by a relative error of at most 0.0003.
Values sent between devices are 32-bit elements; how exact they have to be, the bound alone decides.
A program may use at most 64 MiB of HBM per device.

v0:
```python
import functools
import math

import jax
import jax.numpy as jnp
from jax import lax
from jax.experimental import pallas as pl
from jax.experimental.pallas import tpu as pltpu
from jax.sharding import PartitionSpec as P

ITERS = 2
EPSILON = 1e-06
THETA_START = 0.3

MESH = pl.DeviceIdType.MESH
F32 = jnp.float32
BF16 = jnp.bfloat16
WIDE = 256
PHASES = 3 * ITERS + 1
GROUP = 8
ROUNDS = 3


def theta_after(theta_value):
    return 0.5 * (
        -theta_value * theta_value + theta_value * math.sqrt(theta_value * theta_value + 4.0)
    )


def momentum_factors(iteration_count):
    thetas = [THETA_START]
    for iteration in range(iteration_count):
        thetas.append(theta_after(thetas[-1]))
    return [
        thetas[position]
        * (1.0 - thetas[position])
        / (thetas[position] * thetas[position] + thetas[position + 1])
        for position in range(iteration_count)
    ]


def halves(rows):
    high = rows.astype(BF16).astype(F32)
    return jnp.concatenate([high, rows - high], axis=0).astype(BF16)


def set_hot(index, hot_ref, mask_ref):
    lane = jnp.where(index < 0, -1, index & (WIDE - 1))
    tile = index >> 8
    width = index.shape[1]
    for start in range(0, width, WIDE):
        part = lane[:, start : start + WIDE]
        row = lax.broadcasted_iota(jnp.int32, (WIDE, WIDE), 0)
        hot_ref[:, start : start + WIDE] = (row == part).astype(F32).astype(BF16)
    for number in range(mask_ref.shape[0]):
        mask = (tile == number).astype(F32)
        mask_ref[number] = jnp.broadcast_to(mask, (16, width)).astype(BF16)


def scatter(rows, hot_ref, mask_ref):
    both = halves(rows)
    tiles = mask_ref.shape[0]
    left = jnp.concatenate([both * mask_ref[number] for number in range(tiles)], axis=0)
    sums = lax.dot_general(
        left, hot_ref[...], (((1,), (1,)), ((), ())), preferred_element_type=F32
    )
    return [
        sums[16 * number : 16 * number + 8] + sums[16 * number + 8 : 16 * number + 16]
        for number in range(tiles)
    ]


def gather(tiles, numbers, hot_ref, mask_ref):
    left = jnp.concatenate([halves(tile) for tile in tiles], axis=0)
    found = jnp.dot(left, hot_ref[...], preferred_element_type=F32)
    total = None
    for position, number in enumerate(numbers):
        part = found[16 * position : 16 * position + 8] + found[16 * position + 8 : 16 * position + 16]
        part = part * mask_ref[number][:8].astype(F32)
        total = part if total is None else total + part
    return total


def lanes(row):
    total = row[:, :128]
    for start in range(128, row.shape[1], 128):
        total = total + row[:, start : start + 128]
    return total


def cone_project(normal, first, second, friction):
    slide = jnp.sqrt(first * first + second * second)
    inside = slide <= friction * normal
    polar = friction * slide <= -normal
    outside = jnp.logical_not(jnp.logical_or(inside, polar))
    onto = (friction * slide + normal) / (friction * friction + 1.0)
    scale = friction * onto / jnp.where(outside, slide, 1.0)
    scale = jnp.where(inside, 1.0, jnp.where(polar, 0.0, scale))
    new_normal = jnp.where(inside, normal, jnp.where(polar, 0.0, onto))
    return [new_normal, scale * first, scale * second]


def kernel(
    layers,
    cells,
    free_ref,
    mass_ref,
    jacobian_ref,
    impulses_ref,
    previous_ref,
    compliance_ref,
    offset_ref,
    friction_ref,
    near_ref,
    far_ref,
    counts_ref,
    layer_ref,
    side_ref,
    impulses_out,
    velocity_out,
    near_hot,
    near_mask,
    far_hot,
    far_mask,
    halo_hot,
    halo_mask,
    near_jac,
    far_jac,
    side_out,
    side_in,
    sent,
    received,
    sum_out,
    sum_in,
    side_sems,
    phase_send,
    phase_recv,
    sum_send,
    sum_recv,
):
    g = lax.axis_index("gz")
    x = lax.axis_index("xy")
    below, above = (g + layers - 1) % layers, (g + 1) % layers
    lower, higher = (x + cells - 1) % cells, (x + 1) % cells
    block = x // GROUP * GROUP
    peers = [
        [((g + step) % layers, x) for step in range(1, layers)],
        [(g, block + (x - block + step) % GROUP) for step in range(1, GROUP)],
        [(g, (x + GROUP * step) % cells) for step in range(1, cells // GROUP)],
    ]
    around = [
        (g, lower),
        (g, higher),
        (below, x),
        (above, x),
        (below, lower),
        (below, higher),
        (above, lower),
        (above, higher),
    ]

    barrier = pltpu.get_barrier_semaphore()
    greeted = around + peers[0] + peers[1] + peers[2]
    for device in greeted:
        pl.semaphore_signal(barrier, inc=1, device_id=device, device_id_type=MESH)

    def remote(src, dst, send_sem, recv_sem, device):
        copy = pltpu.make_async_remote_copy(
            src_ref=src,
            dst_ref=dst,
            send_sem=send_sem,
            recv_sem=recv_sem,
            device_id=device,
            device_id_type=MESH,
        )
        copy.start()

    near_jac[...] = jnp.zeros_like(near_jac)
    far_jac[...] = jnp.zeros_like(far_jac)
    for r in range(3):
        near_jac[r, 0:6, :] = jacobian_ref[12 * r : 12 * r + 6, :]
        far_jac[r, 0:6, :] = jacobian_ref[12 * r + 6 : 12 * r + 12, :]
    side_rows = side_ref.shape[1]
    side_list = side_ref[...].astype(F32)
    pad = jnp.full((1, WIDE - side_rows), -1.0, F32)
    side_row = jnp.concatenate([side_list[0:1], pad, side_list[1:2], pad], axis=1)
    side_out[...] = jnp.broadcast_to(side_row, side_out.shape)

    pl.semaphore_wait(barrier, len(greeted))
    remote(side_out, side_in, side_sems.at[0], side_sems.at[1], (above, x))

    own = free_ref.shape[1]
    layer_rows = layer_ref.shape[1]
    section = own + layer_rows
    far = far_ref[...]
    far = jnp.where(
        far < section, far, jnp.where(far < section + side_rows, far + (3 * WIDE - section), far + (4 * WIDE - section - side_rows))
    )
    set_hot(far, far_hot, far_mask)
    set_hot(near_ref[...], near_hot, near_mask)

    slot = lax.broadcasted_iota(jnp.int32, (1, 128), 1)
    alive = jnp.concatenate(
        [(slot < counts_ref[b]).astype(F32) for b in range(counts_ref.shape[0])], axis=1
    )
    softness = compliance_ref[...]
    friction = friction_ref[...]
    offset = offset_ref[...]
    sphere_row = lax.broadcasted_iota(jnp.int32, (8, own), 0)
    weights = jnp.where(
        sphere_row < 3, mass_ref[0:1, :], jnp.where(sphere_row < 6, mass_ref[1:2, :], 0.0)
    )
    free = jnp.concatenate([free_ref[...], jnp.zeros((2, own), F32)], axis=0)

    def set_halo():
        pltpu.make_async_copy(side_in, side_in, side_sems.at[1]).wait()
        layer = layer_ref[...]
        other = side_in[0:1, :].astype(jnp.int32)
        relative = other - own
        row = lax.broadcasted_iota(jnp.int32, (layer_rows, 2 * WIDE), 0)
        hot = (row == relative).astype(F32).astype(BF16)
        parts = jnp.concatenate(
            [jnp.broadcast_to(layer >> 8, (8, layer_rows)), jnp.broadcast_to(layer & 255, (8, layer_rows))], axis=0
        )
        found = jnp.dot(parts.astype(F32).astype(BF16), hot, preferred_element_type=F32)
        composed = (found[0:1] * 256.0 + found[8:9]).astype(jnp.int32)
        composed = jnp.where(relative >= 0, composed, -1)
        mine = side_row.astype(jnp.int32)
        mine = jnp.where(mine < own, mine, -1)
        bottom, first, last = g == 0, x == 0, x == cells - 1
        none = jnp.full((1, WIDE), -1, jnp.int32)
        to_layer = jnp.concatenate([layer, jnp.full((1, WIDE - layer_rows), -1, jnp.int32)], axis=1)
        index = jnp.concatenate(
            [
                jnp.where(bottom, none, to_layer),
                jnp.where(first, none, mine[:, :WIDE]),
                jnp.where(last, none, mine[:, WIDE:]),
                jnp.where(jnp.logical_or(bottom, first), none, composed[:, :WIDE]),
                jnp.where(jnp.logical_or(bottom, last), none, composed[:, WIDE:]),
            ],
            axis=1,
        )
        set_hot(index, halo_hot, halo_mask)

    def part(ref, phase, number):
        return ref.at[phase, :, pl.ds(number * WIDE, WIDE)]

    def arrive(phase):
        pltpu.make_async_copy(received.at[phase], received.at[phase], phase_recv.at[phase]).wait()

    def collect(phase, impulse, between=None):
        far_terms = far_jac[0] * impulse[0] + far_jac[1] * impulse[1] + far_jac[2] * impulse[2]
        far_tiles = scatter(far_terms, far_hot, far_mask)
        for number in range(3):
            sent[phase, :, number * WIDE : (number + 1) * WIDE] = far_tiles[2 + number]
        for number, segment, device in (
            (1, 2, (g, lower)),
            (2, 1, (g, higher)),
            (1, 4, (above, lower)),
            (2, 3, (above, higher)),
            (0, 0, (above, x)),
        ):
            remote(part(sent, phase, number), part(received, phase, segment), phase_send.at[phase], phase_recv.at[phase], device)
        near_terms = near_jac[0] * impulse[0] + near_jac[1] * impulse[1] + near_jac[2] * impulse[2]
        near_tiles = scatter(near_terms, near_hot, near_mask)
        if between is not None:
            between()
        arrive(phase)
        halo_tiles = scatter(received[phase], halo_hot, halo_mask)
        return jnp.concatenate(
            [far_tiles[i] + near_tiles[i] + halo_tiles[i] for i in range(2)], axis=1
        )

    def rows_of(phase, velocity):
        own_tiles = [velocity[:, :WIDE], velocity[:, WIDE:]]
        sent[phase] = gather(own_tiles, range(2), halo_hot, halo_mask)
        for segment, device in (
            (3, (below, lower)),
            (4, (below, higher)),
            (1, (g, lower)),
            (2, (g, higher)),
            (0, (below, x)),
        ):
            remote(part(sent, phase, segment), part(received, phase, segment), phase_send.at[phase], phase_recv.at[phase], device)
        near_rows = gather(own_tiles, range(2), near_hot, near_mask)
        far_rows = gather(own_tiles, range(2), far_hot, far_mask)
        partial = [near_jac[r] * near_rows for r in range(3)]
        arrive(phase)
        segments = [received[phase, :, i * WIDE : (i + 1) * WIDE] for i in range(5)]
        far_rows = far_rows + gather(
            [segments[0], segments[2] + segments[4], segments[1] + segments[3]], (2, 3, 4), far_hot, far_mask
        )
        return [
            jnp.sum(partial[r] + far_jac[r] * far_rows, axis=0, keepdims=True) for r in range(3)
        ]

    def all_sum(iteration, value):
        for number in range(ROUNDS):
            at = iteration * ROUNDS + number
            sum_out[at] = value
            for step, device in enumerate(peers[number]):
                remote(sum_out.at[at], sum_in.at[at, step], sum_send.at[at], sum_recv.at[at], device)
            pltpu.make_async_copy(sum_in.at[at], sum_in.at[at], sum_recv.at[at]).wait()
            for step in range(len(peers[number])):
                value = value + sum_in[at, step]
        return value

    factors = momentum_factors(ITERS)
    current = [alive * impulses_ref[r : r + 1, :] for r in range(3)]
    earlier = [alive * previous_ref[r : r + 1, :] for r in range(3)]
    guess = [alive * (current[r] + factors[0] * (current[r] - earlier[r])) for r in range(3)]
    for iteration in range(ITERS):
        phase = 3 * iteration
        velocity = free + weights * collect(phase, guess, set_halo if iteration == 0 else None)
        rows = rows_of(phase + 1, velocity)
        rows[0] = rows[0] + offset
        gradient = [alive * (rows[r] + softness * guess[r]) for r in range(3)]
        squares = gradient[0] * gradient[0] + gradient[1] * gradient[1] + gradient[2] * gradient[2]
        norm = lanes(squares)
        soft = lanes(softness * squares)
        sums = collect(phase + 2, gradient)
        curve = jnp.sum(lanes(weights * sums * sums), axis=0, keepdims=True) + soft
        tile_row = lax.broadcasted_iota(jnp.int32, (8, 128), 0)
        value = all_sum(iteration, jnp.where(tile_row == 0, norm, curve))
        total = jnp.sum(value, axis=1, keepdims=True)
        step_size = total[0:1] / (total[1:2] + EPSILON)
        moved = [guess[r] - step_size * gradient[r] for r in range(3)]
        updated = [alive * v for v in cone_project(moved[0], moved[1], moved[2], friction)]
        if iteration + 1 < ITERS:
            guess = [
                alive * (updated[r] + factors[iteration + 1] * (updated[r] - current[r]))
                for r in range(3)
            ]
        current = updated
    for r in range(3):
        impulses_out[r : r + 1, :] = current[r]
    final = free + weights * collect(PHASES - 1, current)
    velocity_out[...] = final[0:6, :]

    pltpu.make_async_copy(side_out, side_out, side_sems.at[0]).wait()
    for phase in range(PHASES):
        pltpu.make_async_copy(received.at[phase], received.at[phase], phase_send.at[phase]).wait()
    for at in range(ITERS * ROUNDS):
        pltpu.make_async_copy(sum_in.at[at], sum_in.at[at], sum_send.at[at]).wait()


def solution(mesh):
    layers, cells = mesh.shape["gz"], mesh.shape["xy"]

    def on_device(
        velocity_free,
        inverse_mass,
        jacobian,
        impulses,
        previous_impulses,
        compliance,
        offset,
        friction,
        body_near,
        body_far,
        block_counts,
        layer_send,
        side_send,
    ):
        own = velocity_free.shape[3]
        contacts = jacobian.shape[3]
        vmem = pl.BlockSpec(memory_space=pltpu.VMEM)
        smem = pl.BlockSpec(memory_space=pltpu.SMEM)
        sums = ITERS * ROUNDS
        outs = pl.pallas_call(
            functools.partial(kernel, layers, cells),
            out_shape=(
                jax.ShapeDtypeStruct((3, contacts), F32),
                jax.ShapeDtypeStruct((6, own), F32),
            ),
            in_specs=[vmem] * 10 + [smem] + [vmem] * 2,
            out_specs=(vmem, vmem),
            scratch_shapes=[
                pltpu.VMEM((WIDE, contacts), BF16),
                pltpu.VMEM((2, 16, contacts), BF16),
                pltpu.VMEM((WIDE, contacts), BF16),
                pltpu.VMEM((5, 16, contacts), BF16),
                pltpu.VMEM((WIDE, 5 * WIDE), BF16),
                pltpu.VMEM((2, 16, 5 * WIDE), BF16),
                pltpu.VMEM((3, 8, contacts), F32),
                pltpu.VMEM((3, 8, contacts), F32),
                pltpu.VMEM((8, 2 * WIDE), F32),
                pltpu.VMEM((8, 2 * WIDE), F32),
                pltpu.VMEM((PHASES, 8, 5 * WIDE), F32),
                pltpu.VMEM((PHASES, 8, 5 * WIDE), F32),
                pltpu.VMEM((sums, 8, 128), F32),
                pltpu.VMEM((sums, GROUP - 1, 8, 128), F32),
                pltpu.SemaphoreType.DMA((2,)),
                pltpu.SemaphoreType.DMA((PHASES,)),
                pltpu.SemaphoreType.DMA((PHASES,)),
                pltpu.SemaphoreType.DMA((sums,)),
                pltpu.SemaphoreType.DMA((sums,)),
            ],
            compiler_params=pltpu.CompilerParams(
                collective_id=0, has_side_effects=True, vmem_limit_bytes=40 << 20
            ),
        )(
            velocity_free[0, 0],
            inverse_mass[0, 0],
            jacobian[0, 0],
            impulses[0, 0],
            previous_impulses[0, 0],
            compliance[0],
            offset[0],
            friction[0],
            body_near[0],
            body_far[0],
            block_counts[0, 0],
            layer_send[0],
            side_send[0, 0],
        )
        return outs[0][None, None], outs[1][None, None]

    field = P("gz", "xy", None, None)
    line = P("gz", "xy", None)
    return jax.shard_map(
        on_device,
        mesh=mesh,
        in_specs=(field,) * 5 + (line,) * 7 + (field,),
        out_specs=(field, field),
        check_vma=False,
    )
```

profile of v0, /device:TPU:1, one launch (start us, length us, event | category | flops | bytes accessed | tf_op | source)
XLA Modules:
  0.0 98.5 jit_solution(16630559744754126071)
XLA Ops:
  0.6 0.0 copy-start.9
  0.6 0.7 copy.26
  1.4 0.0 copy-done.9
  1.4 0.8 copy_bitcast_fusion.1
  2.1 0.0 copy-start
  2.1 0.0 copy-start.1
  2.2 0.0 copy-start.2
  2.2 0.0 copy-start.3
  2.2 0.0 copy-start.4
  2.2 0.0 copy-start.5
  2.2 0.0 copy-start.6
  2.2 1.1 %copy.25 = f32[1,1,36,2048]{3,2,1,0:T(8,128)S(1)} copy(f32[1,1,36,2048]{3,1,2,0:T(1,128)} %param.15) | data formatting | bytes 589824
  3.3 0.0 copy-start.7
  3.3 0.0 copy-start.8
  3.3 0.0 copy-done
  3.3 0.0 copy-done.1
  3.4 0.0 copy-done.2
  3.4 0.0 copy-done.3
  3.4 0.0 copy-done.4
  3.4 0.0 copy-done.5
  3.4 0.0 copy-done.6
  3.4 0.6 copy-done.7
  4.0 0.0 copy-done.8
  4.0 93.3 %shard_map.140 = (f32[3,2048]{1,0:T(4,128)S(1)}, f32[6,512]{1,0:T(8,128)S(1)}) custom-call(f32[6,512]{1,0:T(8,128)S(1)} %bitcast.22, f32[2,512]{1,0:T(2,128)S(1)} %bitcast.30, f32[36,2048]{1,0:T(8,128)S(1)} %bitcast.21, f32[3,2048]{1,0:T(4,128)S(1)} %get-tuple-element.9.impulses_ref, f32[3,2048]{1,0:T(4,128)S(1)} %get-tuple-element.8.previous_ref, ...), custom_call_target="tpu_custom_call" | custom-call | tf_op jit(solution)/shard_map/pallas_call | solution.py:370
  97.2 0.6 copy.15
  97.9 0.6 copy.16
Async XLA Ops:
  0.6 0.7 copy-start.9
  2.1 1.2 %copy-start = (f32[1,1,2048]{2,1,0:T(1,128)S(1)}, f32[1,1,2048]{2,1,0:T(1,128)}, u32[]{:S(2)}) copy-start(f32[1,1,2048]{2,1,0:T(1,128)} %param.18) | copy-start | bytes 24580
  2.1 1.2 %copy-start.1 = (f32[1,1,2048]{2,1,0:T(1,128)S(1)}, f32[1,1,2048]{2,1,0:T(1,128)}, u32[]{:S(2)}) copy-start(f32[1,1,2048]{2,1,0:T(1,128)} %param.19) | copy-start | bytes 24580
  2.2 1.2 %copy-start.2 = (f32[1,1,2048]{2,1,0:T(1,128)S(1)}, f32[1,1,2048]{2,1,0:T(1,128)}, u32[]{:S(2)}) copy-start(f32[1,1,2048]{2,1,0:T(1,128)} %param.20) | copy-start | bytes 24580
  2.2 1.2 %copy-start.3 = (s32[1,1,2048]{2,1,0:T(1,128)S(1)}, s32[1,1,2048]{2,1,0:T(1,128)}, u32[]{:S(2)}) copy-start(s32[1,1,2048]{2,1,0:T(1,128)} %param.21) | copy-start | bytes 24580
  2.2 1.2 %copy-start.4 = (s32[1,1,2048]{2,1,0:T(1,128)S(1)}, s32[1,1,2048]{2,1,0:T(1,128)}, u32[]{:S(2)}) copy-start(s32[1,1,2048]{2,1,0:T(1,128)} %param.22) | copy-start | bytes 24580
  2.2 1.2 %copy-start.5 = (f32[1,1,2,512]{3,2,1,0:T(2,128)S(1)}, f32[1,1,2,512]{3,2,1,0:T(2,128)}, u32[]{:S(2)}) copy-start(f32[1,1,2,512]{3,2,1,0:T(2,128)} %param.14) | copy-start | bytes 12292
  2.2 1.2 %copy-start.6 = (s32[1,1,2,192]{3,2,1,0:T(2,128)S(1)}, s32[1,1,2,192]{3,2,1,0:T(2,128)}, u32[]{:S(2)}) copy-start(s32[1,1,2,192]{3,2,1,0:T(2,128)} %param.25) | copy-start | bytes 4612
  3.3 0.7 copy-start.7
  3.3 0.7 copy-start.8
where the time goes:
time: 98.8 us; the launch traced here: 98.5 us
  Pallas kernels  93.3 us (94%)
  local copies, waits for them, and re-layouts  4.46 us (5%)
    pallas_call x1, Pallas kernels, on_device(): pl.pallas_call(functools.partial(kernel, layers, cells), out_shape=(jax.S...  93.3 us
    unnamed x25, local copies, waits for them, and re-layouts  4.46 us

commit v1 on v0

--- a/solution.py
+++ b/solution.py
@@ -17,8 +17,7 @@
 BF16 = jnp.bfloat16
 WIDE = 256
 PHASES = 3 * ITERS + 1
-GROUP = 8
-ROUNDS = 3
+ROUNDS = 2
 
 
 def theta_after(theta_value):
@@ -103,19 +102,20 @@
 def kernel(
     layers,
     cells,
-    free_ref,
-    mass_ref,
-    jacobian_ref,
-    impulses_ref,
-    previous_ref,
-    compliance_ref,
-    offset_ref,
-    friction_ref,
-    near_ref,
-    far_ref,
-    counts_ref,
-    layer_ref,
-    side_ref,
+    depth,
+    free_hbm,
+    mass_hbm,
+    jacobian_hbm,
+    impulses_hbm,
+    previous_hbm,
+    compliance_hbm,
+    offset_hbm,
+    friction_hbm,
+    near_hbm,
+    far_hbm,
+    counts_hbm,
+    layer_hbm,
+    side_hbm,
     impulses_out,
     velocity_out,
     near_hot,
@@ -137,16 +137,34 @@
     phase_recv,
     sum_send,
     sum_recv,
+    free_ref,
+    mass_ref,
+    jacobian_ref,
+    impulses_ref,
+    previous_ref,
+    compliance_ref,
+    offset_ref,
+    friction_ref,
+    near_ref,
+    far_ref,
+    counts_ref,
+    layer_ref,
+    side_ref,
+    load_sems,
 ):
     g = lax.axis_index("gz")
     x = lax.axis_index("xy")
     below, above = (g + layers - 1) % layers, (g + 1) % layers
     lower, higher = (x + cells - 1) % cells, (x + 1) % cells
-    block = x // GROUP * GROUP
+    line = x // depth * depth
     peers = [
-        [((g + step) % layers, x) for step in range(1, layers)],
-        [(g, block + (x - block + step) % GROUP) for step in range(1, GROUP)],
-        [(g, (x + GROUP * step) % cells) for step in range(1, cells // GROUP)],
+        [
+            ((g + step) % layers, (x + depth * stride) % cells)
+            for step in range(layers)
+            for stride in range(cells // depth)
+            if step + stride
+        ],
+        [(g, line + (x - line + step) % depth) for step in range(1, depth)],
     ]
     around = [
         (g, lower),
@@ -159,8 +177,31 @@
         (above, higher),
     ]
 
+    loads = [
+        pltpu.make_async_copy(source, target, load_sems.at[number])
+        for number, (source, target) in enumerate(
+            (
+                (far_hbm, far_ref),
+                (near_hbm, near_ref),
+                (side_hbm, side_ref),
+                (jacobian_hbm, jacobian_ref),
+                (impulses_hbm, impulses_ref),
+                (previous_hbm, previous_ref),
+                (counts_hbm, counts_ref),
+                (layer_hbm, layer_ref),
+                (free_hbm, free_ref),
+                (mass_hbm, mass_ref),
+                (compliance_hbm, compliance_ref),
+                (offset_hbm, offset_ref),
+                (friction_hbm, friction_ref),
+            )
+        )
+    ]
+    for load in loads:
+        load.start()
+
     barrier = pltpu.get_barrier_semaphore()
-    greeted = around + peers[0] + peers[1] + peers[2]
+    greeted = around + peers[0] + peers[1]
     for device in greeted:
         pl.semaphore_signal(barrier, inc=1, device_id=device, device_id_type=MESH)
 
@@ -175,21 +216,23 @@
         )
         copy.start()
 
+    for load in loads:
+        load.wait()
+    slabs = near_jac.shape[2] // 128
     near_jac[...] = jnp.zeros_like(near_jac)
     far_jac[...] = jnp.zeros_like(far_jac)
     for r in range(3):
-        near_jac[r, 0:6, :] = jacobian_ref[12 * r : 12 * r + 6, :]
-        far_jac[r, 0:6, :] = jacobian_ref[12 * r + 6 : 12 * r + 12, :]
+        for t in range(slabs):
+            columns = slice(128 * t, 128 * t + 128)
+            near_jac[r, 0:6, columns] = jacobian_ref[pl.ds(12 * r * slabs + t, 6, slabs), :]
+            far_jac[r, 0:6, columns] = jacobian_ref[pl.ds((12 * r + 6) * slabs + t, 6, slabs), :]
     side_rows = side_ref.shape[1]
     side_list = side_ref[...].astype(F32)
     pad = jnp.full((1, WIDE - side_rows), -1.0, F32)
     side_row = jnp.concatenate([side_list[0:1], pad, side_list[1:2], pad], axis=1)
     side_out[...] = jnp.broadcast_to(side_row, side_out.shape)
 
-    pl.semaphore_wait(barrier, len(greeted))
-    remote(side_out, side_in, side_sems.at[0], side_sems.at[1], (above, x))
-
-    own = free_ref.shape[1]
+    own = free_ref.shape[2]
     layer_rows = layer_ref.shape[1]
     section = own + layer_rows
     far = far_ref[...]
@@ -199,9 +242,13 @@
     set_hot(far, far_hot, far_mask)
     set_hot(near_ref[...], near_hot, near_mask)
 
+    pl.semaphore_wait(barrier, len(greeted))
+    remote(side_out, side_in, side_sems.at[0], side_sems.at[1], (above, x))
+
     slot = lax.broadcasted_iota(jnp.int32, (1, 128), 1)
+    counts = counts_ref[...]
     alive = jnp.concatenate(
-        [(slot < counts_ref[b]).astype(F32) for b in range(counts_ref.shape[0])], axis=1
+        [(slot < counts[:, b : b + 1]).astype(F32) for b in range(counts.shape[1])], axis=1
     )
     softness = compliance_ref[...]
     friction = friction_ref[...]
@@ -210,7 +257,7 @@
     weights = jnp.where(
         sphere_row < 3, mass_ref[0:1, :], jnp.where(sphere_row < 6, mass_ref[1:2, :], 0.0)
     )
-    free = jnp.concatenate([free_ref[...], jnp.zeros((2, own), F32)], axis=0)
+    free = jnp.concatenate([free_ref[j] for j in range(6)] + [jnp.zeros((2, own), F32)], axis=0)
 
     def set_halo():
         pltpu.make_async_copy(side_in, side_in, side_sems.at[1]).wait()
@@ -254,10 +301,10 @@
         for number in range(3):
             sent[phase, :, number * WIDE : (number + 1) * WIDE] = far_tiles[2 + number]
         for number, segment, device in (
+            (1, 4, (above, lower)),
+            (2, 3, (above, higher)),
             (1, 2, (g, lower)),
             (2, 1, (g, higher)),
-            (1, 4, (above, lower)),
-            (2, 3, (above, higher)),
             (0, 0, (above, x)),
         ):
             remote(part(sent, phase, number), part(received, phase, segment), phase_send.at[phase], phase_recv.at[phase], device)
@@ -297,17 +344,22 @@
     def all_sum(iteration, value):
         for number in range(ROUNDS):
             at = iteration * ROUNDS + number
+            count = len(peers[number])
             sum_out[at] = value
             for step, device in enumerate(peers[number]):
                 remote(sum_out.at[at], sum_in.at[at, step], sum_send.at[at], sum_recv.at[at], device)
-            pltpu.make_async_copy(sum_in.at[at], sum_in.at[at], sum_recv.at[at]).wait()
-            for step in range(len(peers[number])):
-                value = value + sum_in[at, step]
+            landed = sum_in.at[at, pl.ds(0, count)]
+            pltpu.make_async_copy(landed, landed, sum_recv.at[at]).wait()
+            terms = [value] + [sum_in[at, step] for step in range(count)]
+            while len(terms) > 1:
+                pairs = [a + b for a, b in zip(terms[::2], terms[1::2])]
+                terms = pairs + terms[2 * len(pairs) :]
+            value = terms[0]
         return value
 
     factors = momentum_factors(ITERS)
-    current = [alive * impulses_ref[r : r + 1, :] for r in range(3)]
-    earlier = [alive * previous_ref[r : r + 1, :] for r in range(3)]
+    current = [alive * impulses_ref[r] for r in range(3)]
+    earlier = [alive * previous_ref[r] for r in range(3)]
     guess = [alive * (current[r] + factors[0] * (current[r] - earlier[r])) for r in range(3)]
     for iteration in range(ITERS):
         phase = 3 * iteration
@@ -320,8 +372,7 @@
         soft = lanes(softness * squares)
         sums = collect(phase + 2, gradient)
         curve = jnp.sum(lanes(weights * sums * sums), axis=0, keepdims=True) + soft
-        tile_row = lax.broadcasted_iota(jnp.int32, (8, 128), 0)
-        value = all_sum(iteration, jnp.where(tile_row == 0, norm, curve))
+        value = all_sum(iteration, jnp.concatenate([norm, curve], axis=0))
         total = jnp.sum(value, axis=1, keepdims=True)
         step_size = total[0:1] / (total[1:2] + EPSILON)
         moved = [guess[r] - step_size * gradient[r] for r in range(3)]
@@ -333,19 +384,22 @@
             ]
         current = updated
     for r in range(3):
-        impulses_out[r : r + 1, :] = current[r]
+        impulses_out[r] = current[r]
     final = free + weights * collect(PHASES - 1, current)
-    velocity_out[...] = final[0:6, :]
+    for j in range(6):
+        velocity_out[j] = final[j : j + 1, :]
 
     pltpu.make_async_copy(side_out, side_out, side_sems.at[0]).wait()
     for phase in range(PHASES):
         pltpu.make_async_copy(received.at[phase], received.at[phase], phase_send.at[phase]).wait()
     for at in range(ITERS * ROUNDS):
-        pltpu.make_async_copy(sum_in.at[at], sum_in.at[at], sum_send.at[at]).wait()
+        gone = sum_in.at[at, pl.ds(0, len(peers[at % ROUNDS]))]
+        pltpu.make_async_copy(gone, gone, sum_send.at[at]).wait()
 
 
 def solution(mesh):
     layers, cells = mesh.shape["gz"], mesh.shape["xy"]
+    depth = 16
 
     def on_device(
         velocity_free,
@@ -365,15 +419,30 @@
         own = velocity_free.shape[3]
         contacts = jacobian.shape[3]
         vmem = pl.BlockSpec(memory_space=pltpu.VMEM)
-        smem = pl.BlockSpec(memory_space=pltpu.SMEM)
         sums = ITERS * ROUNDS
+        partners = max(layers * (cells // depth), depth) - 1
+        operands = (
+            velocity_free.reshape(6, 1, own),
+            inverse_mass[0, 0],
+            jacobian.reshape(36 * contacts // 128, 128),
+            impulses.reshape(3, 1, contacts),
+            previous_impulses.reshape(3, 1, contacts),
+            compliance[0],
+            offset[0],
+            friction[0],
+            body_near[0],
+            body_far[0],
+            block_counts[0],
+            layer_send[0],
+            side_send[0, 0],
+        )
         outs = pl.pallas_call(
-            functools.partial(kernel, layers, cells),
+            functools.partial(kernel, layers, cells, depth),
             out_shape=(
-                jax.ShapeDtypeStruct((3, contacts), F32),
-                jax.ShapeDtypeStruct((6, own), F32),
+                jax.ShapeDtypeStruct((3, 1, contacts), F32),
+                jax.ShapeDtypeStruct((6, 1, own), F32),
             ),
-            in_specs=[vmem] * 10 + [smem] + [vmem] * 2,
+            in_specs=[pl.BlockSpec(memory_space=pl.ANY)] * 13,
             out_specs=(vmem, vmem),
             scratch_shapes=[
                 pltpu.VMEM((WIDE, contacts), BF16),
@@ -388,33 +457,21 @@
                 pltpu.VMEM((8, 2 * WIDE), F32),
                 pltpu.VMEM((PHASES, 8, 5 * WIDE), F32),
                 pltpu.VMEM((PHASES, 8, 5 * WIDE), F32),
-                pltpu.VMEM((sums, 8, 128), F32),
-                pltpu.VMEM((sums, GROUP - 1, 8, 128), F32),
+                pltpu.VMEM((sums, 2, 128), F32),
+                pltpu.VMEM((sums, partners, 2, 128), F32),
                 pltpu.SemaphoreType.DMA((2,)),
                 pltpu.SemaphoreType.DMA((PHASES,)),
                 pltpu.SemaphoreType.DMA((PHASES,)),
                 pltpu.SemaphoreType.DMA((sums,)),
                 pltpu.SemaphoreType.DMA((sums,)),
+                *[pltpu.VMEM(v.shape, v.dtype) for v in operands],
+                pltpu.SemaphoreType.DMA((len(operands),)),
             ],
             compiler_params=pltpu.CompilerParams(
-                collective_id=0, has_side_effects=True, vmem_limit_bytes=40 << 20
+                collective_id=0, has_side_effects=True, vmem_limit_bytes=56 << 20
             ),
-        )(
-            velocity_free[0, 0],
-            inverse_mass[0, 0],
-            jacobian[0, 0],
-            impulses[0, 0],
-            previous_impulses[0, 0],
-            compliance[0],
-            offset[0],
-            friction[0],
-            body_near[0],
-            body_far[0],
-            block_counts[0, 0],
-            layer_send[0],
-            side_send[0, 0],
-        )
-        return outs[0][None, None], outs[1][None, None]
+        )(*operands)
+        return outs[0].reshape(1, 1, 3, contacts), outs[1].reshape(1, 1, 6, own)
 
     field = P("gz", "xy", None, None)
     line = P("gz", "xy", None)

time: 98.8 us -> 79.6 us (0.81)
  Pallas kernels: 93.3 us -> 76.8 us
  local copies, waits for them, and re-layouts: 4.46 us -> 1.96 us
    pallas_call x1, Pallas kernels: 93.3 us -> 76.8 us  [on_device(): pl.pallas_call(functools.partial(kernel, layers, cells, depth), out_shape...]
    unnamed x25 -> x4, local copies, waits for them, and re-layouts: 4.46 us -> 1.96 us
where the time goes in v1:
time: 79.6 us; the launch traced here: 79.4 us
  Pallas kernels  76.8 us (96%)
  local copies, waits for them, and re-layouts  1.96 us (2%)
    pallas_call x1, Pallas kernels, on_device(): pl.pallas_call(functools.partial(kernel, layers, cells, depth), out_shape...  76.8 us
    unnamed x4, local copies, waits for them, and re-layouts  1.96 us

profile of v1, /device:TPU:1, one launch (start us, length us, event | category | flops | bytes accessed | tf_op | source)
XLA Modules:
  0.0 79.4 jit_solution(524424329440260931)
XLA Ops:
  0.6 76.8 %shard_map.140 = (f32[3,1,2048]{2,1,0:T(1,128)}, f32[6,1,512]{2,1,0:T(1,128)}) custom-call(f32[6,1,512]{2,1,0:T(1,128)} %bitcast.23, f32[2,512]{1,0:T(2,128)} %bitcast.30, f32[576,128]{1,0:T(8,128)} %bitcast.19, f32[3,1,2048]{2,1,0:T(1,128)} %bitcast.20, f32[3,1,2048]{2,1,0:T(1,128)} %bitcast.21, f32[1,2048]{1,0:T(1,128)} %bitcast.25, f32[1,2048]{1,0:T(1,128)} %bitcast.26, ...), custom_call_target="tpu_custom_call" | custom-call | tf_op jit(solution)/shard_map/pallas_call | solution.py:439
  77.5 0.0 copy-start
  77.5 1.4 %copy.19 = f32[1,1,3,2048]{3,1,2,0:T(1,128)} copy(f32[1,1,3,2048]{3,1,2,0:T(1,128)} %bitcast.22) | data formatting | bytes 49152
  78.8 0.0 copy-done
  78.8 0.6 copy.20
Async XLA Ops:
  77.5 1.4 %copy-start = (f32[6,1,512]{2,1,0:T(1,128)S(1)}, f32[6,1,512]{2,1,0:T(1,128)}, u32[]{:S(2)}) copy-start(f32[6,1,512]{2,1,0:T(1,128)} %get-tuple-element.5) | copy-start | bytes 36868

commit v2 on v1

--- a/solution.py
+++ b/solution.py
@@ -17,6 +17,7 @@
 BF16 = jnp.bfloat16
 WIDE = 256
 PHASES = 3 * ITERS + 1
+SPREADS = tuple(3 * iteration + 1 for iteration in range(ITERS))
 ROUNDS = 2
 
 
@@ -137,6 +138,7 @@
     phase_recv,
     sum_send,
     sum_recv,
+    token_sems,
     free_ref,
     mass_ref,
     jacobian_ref,
@@ -154,6 +156,11 @@
 ):
     g = lax.axis_index("gz")
     x = lax.axis_index("xy")
+    has_below, has_above = g > 0, g < layers - 1
+    has_lower, has_higher = x > 0, x < cells - 1
+    beside = has_lower.astype(jnp.int32) + has_higher.astype(jnp.int32)
+    upward = beside + jnp.where(has_above, beside + 1, 0)
+    downward = beside + jnp.where(has_below, beside + 1, 0)
     below, above = (g + layers - 1) % layers, (g + 1) % layers
     lower, higher = (x + cells - 1) % cells, (x + 1) % cells
     line = x // depth * depth
@@ -200,8 +207,14 @@
     for load in loads:
         load.start()
 
+    received[...] = jnp.zeros_like(received)
+    side_in[...] = jnp.full_like(side_in, -1.0)
+
     barrier = pltpu.get_barrier_semaphore()
-    greeted = around + peers[0] + peers[1]
+    def along(step):
+        return (g, line + (x - line + step) % depth)
+
+    greeted = around + peers[0] + [along(step) for step in (1, 2, depth - 1, depth - 2)]
     for device in greeted:
         pl.semaphore_signal(barrier, inc=1, device_id=device, device_id_type=MESH)
 
@@ -243,7 +256,9 @@
     set_hot(near_ref[...], near_hot, near_mask)
 
     pl.semaphore_wait(barrier, len(greeted))
-    remote(side_out, side_in, side_sems.at[0], side_sems.at[1], (above, x))
+    @pl.when(has_above)
+    def _():
+        remote(side_out, side_in, side_sems.at[0], side_sems.at[1], (above, x))
 
     slot = lax.broadcasted_iota(jnp.int32, (1, 128), 1)
     counts = counts_ref[...]
@@ -260,7 +275,10 @@
     free = jnp.concatenate([free_ref[j] for j in range(6)] + [jnp.zeros((2, own), F32)], axis=0)
 
     def set_halo():
-        pltpu.make_async_copy(side_in, side_in, side_sems.at[1]).wait()
+        @pl.when(has_below)
+        def _():
+            pltpu.make_async_copy(side_in, side_in, side_sems.at[1]).wait()
+
         layer = layer_ref[...]
         other = side_in[0:1, :].astype(jnp.int32)
         relative = other - own
@@ -292,27 +310,46 @@
     def part(ref, phase, number):
         return ref.at[phase, :, pl.ds(number * WIDE, WIDE)]
 
-    def arrive(phase):
-        pltpu.make_async_copy(received.at[phase], received.at[phase], phase_recv.at[phase]).wait()
+    def pass_token(number):
+        for step in (2 << number, depth - (2 << number)):
+            pl.semaphore_signal(
+                token_sems.at[number], inc=1, device_id=along(step), device_id_type=MESH
+            )
+
+    def send(phase, number, segment, device, valid):
+        @pl.when(valid)
+        def _():
+            remote(
+                part(sent, phase, number),
+                part(received, phase, segment),
+                phase_send.at[phase],
+                phase_recv.at[phase],
+                device,
+            )
+
+    def await_segments(phase, sem, count):
+        for number in (1, 2, 3, 5):
+
+            @pl.when(count == number)
+            def _():
+                moved = received.at[phase, :, pl.ds(0, number * WIDE)]
+                pltpu.make_async_copy(moved, moved, sem.at[phase]).wait()
 
     def collect(phase, impulse, between=None):
         far_terms = far_jac[0] * impulse[0] + far_jac[1] * impulse[1] + far_jac[2] * impulse[2]
         far_tiles = scatter(far_terms, far_hot, far_mask)
         for number in range(3):
             sent[phase, :, number * WIDE : (number + 1) * WIDE] = far_tiles[2 + number]
-        for number, segment, device in (
-            (1, 4, (above, lower)),
-            (2, 3, (above, higher)),
-            (1, 2, (g, lower)),
-            (2, 1, (g, higher)),
-            (0, 0, (above, x)),
-        ):
-            remote(part(sent, phase, number), part(received, phase, segment), phase_send.at[phase], phase_recv.at[phase], device)
+        send(phase, 1, 4, (above, lower), jnp.logical_and(has_above, has_lower))
+        send(phase, 2, 3, (above, higher), jnp.logical_and(has_above, has_higher))
+        send(phase, 1, 2, (g, lower), has_lower)
+        send(phase, 2, 1, (g, higher), has_higher)
+        send(phase, 0, 0, (above, x), has_above)
         near_terms = near_jac[0] * impulse[0] + near_jac[1] * impulse[1] + near_jac[2] * impulse[2]
         near_tiles = scatter(near_terms, near_hot, near_mask)
         if between is not None:
             between()
-        arrive(phase)
+        await_segments(phase, phase_recv, downward)
         halo_tiles = scatter(received[phase], halo_hot, halo_mask)
         return jnp.concatenate(
             [far_tiles[i] + near_tiles[i] + halo_tiles[i] for i in range(2)], axis=1
@@ -321,18 +358,15 @@
     def rows_of(phase, velocity):
         own_tiles = [velocity[:, :WIDE], velocity[:, WIDE:]]
         sent[phase] = gather(own_tiles, range(2), halo_hot, halo_mask)
-        for segment, device in (
-            (3, (below, lower)),
-            (4, (below, higher)),
-            (1, (g, lower)),
-            (2, (g, higher)),
-            (0, (below, x)),
-        ):
-            remote(part(sent, phase, segment), part(received, phase, segment), phase_send.at[phase], phase_recv.at[phase], device)
+        send(phase, 3, 3, (below, lower), jnp.logical_and(has_below, has_lower))
+        send(phase, 4, 4, (below, higher), jnp.logical_and(has_below, has_higher))
+        send(phase, 1, 1, (g, lower), has_lower)
+        send(phase, 2, 2, (g, higher), has_higher)
+        send(phase, 0, 0, (below, x), has_below)
         near_rows = gather(own_tiles, range(2), near_hot, near_mask)
         far_rows = gather(own_tiles, range(2), far_hot, far_mask)
         partial = [near_jac[r] * near_rows for r in range(3)]
-        arrive(phase)
+        await_segments(phase, phase_recv, upward)
         segments = [received[phase, :, i * WIDE : (i + 1) * WIDE] for i in range(5)]
         far_rows = far_rows + gather(
             [segments[0], segments[2] + segments[4], segments[1] + segments[3]], (2, 3, 4), far_hot, far_mask
@@ -357,6 +391,7 @@
             value = terms[0]
         return value
 
+    pass_token(0)
     factors = momentum_factors(ITERS)
     current = [alive * impulses_ref[r] for r in range(3)]
     earlier = [alive * previous_ref[r] for r in range(3)]
@@ -364,6 +399,9 @@
     for iteration in range(ITERS):
         phase = 3 * iteration
         velocity = free + weights * collect(phase, guess, set_halo if iteration == 0 else None)
+        if iteration == 0:
+            pl.semaphore_wait(token_sems.at[0], 2)
+            pass_token(1)
         rows = rows_of(phase + 1, velocity)
         rows[0] = rows[0] + offset
         gradient = [alive * (rows[r] + softness * guess[r]) for r in range(3)]
@@ -371,6 +409,8 @@
         norm = lanes(squares)
         soft = lanes(softness * squares)
         sums = collect(phase + 2, gradient)
+        if iteration == 0:
+            pl.semaphore_wait(token_sems.at[1], 2)
         curve = jnp.sum(lanes(weights * sums * sums), axis=0, keepdims=True) + soft
         value = all_sum(iteration, jnp.concatenate([norm, curve], axis=0))
         total = jnp.sum(value, axis=1, keepdims=True)
@@ -389,9 +429,12 @@
     for j in range(6):
         velocity_out[j] = final[j : j + 1, :]
 
-    pltpu.make_async_copy(side_out, side_out, side_sems.at[0]).wait()
+    @pl.when(has_above)
+    def _():
+        pltpu.make_async_copy(side_out, side_out, side_sems.at[0]).wait()
+
     for phase in range(PHASES):
-        pltpu.make_async_copy(received.at[phase], received.at[phase], phase_send.at[phase]).wait()
+        await_segments(phase, phase_send, downward if phase in SPREADS else upward)
     for at in range(ITERS * ROUNDS):
         gone = sum_in.at[at, pl.ds(0, len(peers[at % ROUNDS]))]
         pltpu.make_async_copy(gone, gone, sum_send.at[at]).wait()
@@ -464,6 +507,7 @@
                 pltpu.SemaphoreType.DMA((PHASES,)),
                 pltpu.SemaphoreType.DMA((sums,)),
                 pltpu.SemaphoreType.DMA((sums,)),
+                pltpu.SemaphoreType.REGULAR((2,)),
                 *[pltpu.VMEM(v.shape, v.dtype) for v in operands],
                 pltpu.SemaphoreType.DMA((len(operands),)),
             ],

time: 79.6 us -> 73.6 us (0.925)
  Pallas kernels: 76.8 us -> 70.3 us
    pallas_call x1, Pallas kernels: 76.8 us -> 70.3 us  [on_device(): pl.pallas_call(functools.partial(kernel, layers, cells, depth), out_shape...]
where the time goes in v2:
time: 73.6 us; the launch traced here: 73 us
  Pallas kernels  70.3 us (96%)
  local copies, waits for them, and re-layouts  1.96 us (3%)
    pallas_call x1, Pallas kernels, on_device(): pl.pallas_call(functools.partial(kernel, layers, cells, depth), out_shape...  70.3 us
    unnamed x4, local copies, waits for them, and re-layouts  1.96 us

profile of v2, /device:TPU:1, one launch (start us, length us, event | category | flops | bytes accessed | tf_op | source)
XLA Modules:
  0.0 73.0 jit_solution(3220091616017829961)
XLA Ops:
  0.6 70.3 %shard_map.140 = (f32[3,1,2048]{2,1,0:T(1,128)}, f32[6,1,512]{2,1,0:T(1,128)}) custom-call(f32[6,1,512]{2,1,0:T(1,128)} %bitcast.23, f32[2,512]{1,0:T(2,128)} %bitcast.30, f32[576,128]{1,0:T(8,128)} %bitcast.19, f32[3,1,2048]{2,1,0:T(1,128)} %bitcast.20, f32[3,1,2048]{2,1,0:T(1,128)} %bitcast.21, f32[1,2048]{1,0:T(1,128)} %bitcast.25, f32[1,2048]{1,0:T(1,128)} %bitcast.26, ...), custom_call_target="tpu_custom_call" | custom-call | tf_op jit(solution)/shard_map/pallas_call | solution.py:482
  71.0 0.0 copy-start
  71.0 1.4 %copy.19 = f32[1,1,3,2048]{3,1,2,0:T(1,128)} copy(f32[1,1,3,2048]{3,1,2,0:T(1,128)} %bitcast.22) | data formatting | bytes 49152
  72.3 0.0 copy-done
  72.4 0.6 copy.20
Async XLA Ops:
  71.0 1.4 %copy-start = (f32[6,1,512]{2,1,0:T(1,128)S(1)}, f32[6,1,512]{2,1,0:T(1,128)}, u32[]{:S(2)}) copy-start(f32[6,1,512]{2,1,0:T(1,128)} %get-tuple-element.5) | copy-start | bytes 36868

commit v3 on v2

--- a/solution.py
+++ b/solution.py
@@ -57,16 +57,14 @@
         mask_ref[number] = jnp.broadcast_to(mask, (16, width)).astype(BF16)
 
 
-def scatter(rows, hot_ref, mask_ref):
-    both = halves(rows)
-    tiles = mask_ref.shape[0]
-    left = jnp.concatenate([both * mask_ref[number] for number in range(tiles)], axis=0)
+def scatter(both, numbers, hot_ref, mask_ref):
+    left = jnp.concatenate([both * mask_ref[number] for number in numbers], axis=0)
     sums = lax.dot_general(
         left, hot_ref[...], (((1,), (1,)), ((), ())), preferred_element_type=F32
     )
     return [
-        sums[16 * number : 16 * number + 8] + sums[16 * number + 8 : 16 * number + 16]
-        for number in range(tiles)
+        sums[16 * i : 16 * i + 8] + sums[16 * i + 8 : 16 * i + 16]
+        for i in range(len(numbers))
     ]
 
 
@@ -167,11 +165,11 @@
     peers = [
         [
             ((g + step) % layers, (x + depth * stride) % cells)
-            for step in range(layers)
-            for stride in range(cells // depth)
+            for step in sorted(range(layers), key=lambda step: -min(step, layers - step))
+            for stride in (2, 1, 3, 0)
             if step + stride
         ],
-        [(g, line + (x - line + step) % depth) for step in range(1, depth)],
+        [(g, line + (x - line + step) % depth) for step in sorted(range(1, depth), key=lambda step: -min(step, depth - step))],
     ]
     around = [
         (g, lower),
@@ -214,7 +212,18 @@
     def along(step):
         return (g, line + (x - line + step) % depth)
 
-    greeted = around + peers[0] + [along(step) for step in (1, 2, depth - 1, depth - 2)]
+    def across(step):
+        return (g, (x + depth * step) % cells)
+
+    def through(step):
+        return ((g + step) % layers, x)
+
+    both_ways = lambda place, *steps: [place(step) for near in steps for step in (near, -near)]
+    greeted = around + both_ways(through, 2) + both_ways(across, 1) + both_ways(along, 1, 2)
+    tokens = [
+        both_ways(through, 2) + both_ways(across, 1) + both_ways(along, 2),
+        both_ways(across, 1) + [across(2)] + both_ways(along, 4),
+    ]
     for device in greeted:
         pl.semaphore_signal(barrier, inc=1, device_id=device, device_id_type=MESH)
 
@@ -311,10 +320,8 @@
         return ref.at[phase, :, pl.ds(number * WIDE, WIDE)]
 
     def pass_token(number):
-        for step in (2 << number, depth - (2 << number)):
-            pl.semaphore_signal(
-                token_sems.at[number], inc=1, device_id=along(step), device_id_type=MESH
-            )
+        for device in tokens[number]:
+            pl.semaphore_signal(token_sems.at[number], inc=1, device_id=device, device_id_type=MESH)
 
     def send(phase, number, segment, device, valid):
         @pl.when(valid)
@@ -337,20 +344,22 @@
 
     def collect(phase, impulse, between=None):
         far_terms = far_jac[0] * impulse[0] + far_jac[1] * impulse[1] + far_jac[2] * impulse[2]
-        far_tiles = scatter(far_terms, far_hot, far_mask)
+        far_terms = halves(far_terms)
+        leaving = scatter(far_terms, (2, 3, 4), far_hot, far_mask)
         for number in range(3):
-            sent[phase, :, number * WIDE : (number + 1) * WIDE] = far_tiles[2 + number]
+            sent[phase, :, number * WIDE : (number + 1) * WIDE] = leaving[number]
         send(phase, 1, 4, (above, lower), jnp.logical_and(has_above, has_lower))
         send(phase, 2, 3, (above, higher), jnp.logical_and(has_above, has_higher))
         send(phase, 1, 2, (g, lower), has_lower)
         send(phase, 2, 1, (g, higher), has_higher)
         send(phase, 0, 0, (above, x), has_above)
         near_terms = near_jac[0] * impulse[0] + near_jac[1] * impulse[1] + near_jac[2] * impulse[2]
-        near_tiles = scatter(near_terms, near_hot, near_mask)
+        near_tiles = scatter(halves(near_terms), (0, 1), near_hot, near_mask)
+        far_tiles = scatter(far_terms, (0, 1), far_hot, far_mask)
         if between is not None:
             between()
         await_segments(phase, phase_recv, downward)
-        halo_tiles = scatter(received[phase], halo_hot, halo_mask)
+        halo_tiles = scatter(halves(received[phase]), (0, 1), halo_hot, halo_mask)
         return jnp.concatenate(
             [far_tiles[i] + near_tiles[i] + halo_tiles[i] for i in range(2)], axis=1
         )
@@ -380,8 +389,20 @@
             at = iteration * ROUNDS + number
             count = len(peers[number])
             sum_out[at] = value
-            for step, device in enumerate(peers[number]):
-                remote(sum_out.at[at], sum_in.at[at, step], sum_send.at[at], sum_recv.at[at], device)
+            def give(devices):
+                for step, device in enumerate(devices):
+                    remote(sum_out.at[at], sum_in.at[at, step], sum_send.at[at], sum_recv.at[at], device)
+
+            if number == 0:
+                give(peers[0])
+            else:
+
+                @pl.when(g % 2 == 1)
+                def _():
+                    for step, (layer, cell) in enumerate(peers[1]):
+                        for target in (layer - 1, layer):
+                            remote(sum_out.at[at], sum_in.at[at, step], sum_send.at[at], sum_recv.at[at], (target, cell))
+
             landed = sum_in.at[at, pl.ds(0, count)]
             pltpu.make_async_copy(landed, landed, sum_recv.at[at]).wait()
             terms = [value] + [sum_in[at, step] for step in range(count)]
@@ -400,7 +421,7 @@
         phase = 3 * iteration
         velocity = free + weights * collect(phase, guess, set_halo if iteration == 0 else None)
         if iteration == 0:
-            pl.semaphore_wait(token_sems.at[0], 2)
+            pl.semaphore_wait(token_sems.at[0], len(tokens[0]))
             pass_token(1)
         rows = rows_of(phase + 1, velocity)
         rows[0] = rows[0] + offset
@@ -410,7 +431,7 @@
         soft = lanes(softness * squares)
         sums = collect(phase + 2, gradient)
         if iteration == 0:
-            pl.semaphore_wait(token_sems.at[1], 2)
+            pl.semaphore_wait(token_sems.at[1], len(tokens[1]))
         curve = jnp.sum(lanes(weights * sums * sums), axis=0, keepdims=True) + soft
         value = all_sum(iteration, jnp.concatenate([norm, curve], axis=0))
         total = jnp.sum(value, axis=1, keepdims=True)
@@ -436,8 +457,11 @@
     for phase in range(PHASES):
         await_segments(phase, phase_send, downward if phase in SPREADS else upward)
     for at in range(ITERS * ROUNDS):
-        gone = sum_in.at[at, pl.ds(0, len(peers[at % ROUNDS]))]
-        pltpu.make_async_copy(gone, gone, sum_send.at[at]).wait()
+        gone = sum_in.at[at, pl.ds(0, len(peers[0]) if at % ROUNDS == 0 else 2 * len(peers[1]))]
+
+        @pl.when(jnp.logical_or(at % ROUNDS == 0, g % 2 == 1))
+        def _():
+            pltpu.make_async_copy(gone, gone, sum_send.at[at]).wait()
 
 
 def solution(mesh):

time: 73.6 us -> 70.2 us (0.954)
  Pallas kernels: 70.3 us -> 67.4 us
    pallas_call x1, Pallas kernels: 70.3 us -> 67.4 us  [on_device(): pl.pallas_call(functools.partial(kernel, layers, cells, depth), out_shape...]
where the time goes in v3:
time: 70.2 us; the launch traced here: 70 us
  Pallas kernels  67.4 us (96%)
  local copies, waits for them, and re-layouts  1.96 us (3%)
    pallas_call x1, Pallas kernels, on_device(): pl.pallas_call(functools.partial(kernel, layers, cells, depth), out_shape...  67.4 us
    unnamed x4, local copies, waits for them, and re-layouts  1.96 us

profile of v3, /device:TPU:1, one launch (start us, length us, event | category | flops | bytes accessed | tf_op | source)
XLA Modules:
  0.0 70.0 jit_solution(13214115035639539957)
XLA Ops:
  0.6 67.4 %shard_map.140 = (f32[3,1,2048]{2,1,0:T(1,128)}, f32[6,1,512]{2,1,0:T(1,128)}) custom-call(f32[6,1,512]{2,1,0:T(1,128)} %bitcast.23, f32[2,512]{1,0:T(2,128)} %bitcast.30, f32[576,128]{1,0:T(8,128)} %bitcast.19, f32[3,1,2048]{2,1,0:T(1,128)} %bitcast.20, f32[3,1,2048]{2,1,0:T(1,128)} %bitcast.21, f32[1,2048]{1,0:T(1,128)} %bitcast.25, f32[1,2048]{1,0:T(1,128)} %bitcast.26, ...), custom_call_target="tpu_custom_call" | custom-call | tf_op jit(solution)/shard_map/pallas_call | solution.py:506
  68.1 0.0 copy-start
  68.1 1.4 %copy.19 = f32[1,1,3,2048]{3,1,2,0:T(1,128)} copy(f32[1,1,3,2048]{3,1,2,0:T(1,128)} %bitcast.22) | data formatting | bytes 49152
  69.4 0.0 copy-done
  69.4 0.6 copy.20
Async XLA Ops:
  68.1 1.4 %copy-start = (f32[6,1,512]{2,1,0:T(1,128)S(1)}, f32[6,1,512]{2,1,0:T(1,128)}, u32[]{:S(2)}) copy-start(f32[6,1,512]{2,1,0:T(1,128)} %get-tuple-element.5) | copy-start | bytes 36868

commit v4 on v3

--- a/solution.py
+++ b/solution.py
@@ -162,14 +162,15 @@
     below, above = (g + layers - 1) % layers, (g + 1) % layers
     lower, higher = (x + cells - 1) % cells, (x + 1) % cells
     line = x // depth * depth
-    peers = [
-        [
-            ((g + step) % layers, (x + depth * stride) % cells)
-            for step in sorted(range(layers), key=lambda step: -min(step, layers - step))
-            for stride in (2, 1, 3, 0)
-            if step + stride
-        ],
-        [(g, line + (x - line + step) % depth) for step in sorted(range(1, depth), key=lambda step: -min(step, depth - step))],
+    odd = g % 2 == 1
+    plane = [
+        ((g // 2 * 2 + 1 + 2 * step) % layers, (x + depth * stride) % cells)
+        for step in (2, 1, 3, 0)
+        for stride in (2, 1, 3, 0)
+    ]
+    column = [
+        (g, line + (x - line + step) % depth)
+        for step in sorted(range(1, depth), key=lambda step: -min(step, depth - step))
     ]
     around = [
         (g, lower),
@@ -262,7 +263,6 @@
         far < section, far, jnp.where(far < section + side_rows, far + (3 * WIDE - section), far + (4 * WIDE - section - side_rows))
     )
     set_hot(far, far_hot, far_mask)
-    set_hot(near_ref[...], near_hot, near_mask)
 
     pl.semaphore_wait(barrier, len(greeted))
     @pl.when(has_above)
@@ -282,6 +282,9 @@
         sphere_row < 3, mass_ref[0:1, :], jnp.where(sphere_row < 6, mass_ref[1:2, :], 0.0)
     )
     free = jnp.concatenate([free_ref[j] for j in range(6)] + [jnp.zeros((2, own), F32)], axis=0)
+
+    def set_near():
+        set_hot(near_ref[...], near_hot, near_mask)
 
     def set_halo():
         @pl.when(has_below)
@@ -342,7 +345,7 @@
                 moved = received.at[phase, :, pl.ds(0, number * WIDE)]
                 pltpu.make_async_copy(moved, moved, sem.at[phase]).wait()
 
-    def collect(phase, impulse, between=None):
+    def collect(phase, impulse, ready=None, between=None):
         far_terms = far_jac[0] * impulse[0] + far_jac[1] * impulse[1] + far_jac[2] * impulse[2]
         far_terms = halves(far_terms)
         leaving = scatter(far_terms, (2, 3, 4), far_hot, far_mask)
@@ -353,6 +356,8 @@
         send(phase, 1, 2, (g, lower), has_lower)
         send(phase, 2, 1, (g, higher), has_higher)
         send(phase, 0, 0, (above, x), has_above)
+        if ready is not None:
+            ready()
         near_terms = near_jac[0] * impulse[0] + near_jac[1] * impulse[1] + near_jac[2] * impulse[2]
         near_tiles = scatter(halves(near_terms), (0, 1), near_hot, near_mask)
         far_tiles = scatter(far_terms, (0, 1), far_hot, far_mask)
@@ -384,33 +389,44 @@
             jnp.sum(partial[r] + far_jac[r] * far_rows, axis=0, keepdims=True) for r in range(3)
         ]
 
+    def tree(terms):
+        while len(terms) > 1:
+            pairs = [a + b for a, b in zip(terms[::2], terms[1::2])]
+            terms = pairs + terms[2 * len(pairs) :]
+        return terms[0]
+
+    def rows_moved(at, sem, count):
+        moved = sum_in.at[at, pl.ds(0, count)]
+        pltpu.make_async_copy(moved, moved, sem.at[at]).wait()
+
+    def give(at, slot, device):
+        remote(sum_out.at[at], sum_in.at[at, slot], sum_send.at[at], sum_recv.at[at], device)
+
     def all_sum(iteration, value):
-        for number in range(ROUNDS):
-            at = iteration * ROUNDS + number
-            count = len(peers[number])
-            sum_out[at] = value
-            def give(devices):
-                for step, device in enumerate(devices):
-                    remote(sum_out.at[at], sum_in.at[at, step], sum_send.at[at], sum_recv.at[at], device)
-
-            if number == 0:
-                give(peers[0])
-            else:
-
-                @pl.when(g % 2 == 1)
-                def _():
-                    for step, (layer, cell) in enumerate(peers[1]):
-                        for target in (layer - 1, layer):
-                            remote(sum_out.at[at], sum_in.at[at, step], sum_send.at[at], sum_recv.at[at], (target, cell))
-
-            landed = sum_in.at[at, pl.ds(0, count)]
-            pltpu.make_async_copy(landed, landed, sum_recv.at[at]).wait()
-            terms = [value] + [sum_in[at, step] for step in range(count)]
-            while len(terms) > 1:
-                pairs = [a + b for a, b in zip(terms[::2], terms[1::2])]
-                terms = pairs + terms[2 * len(pairs) :]
-            value = terms[0]
-        return value
+        at = iteration * ROUNDS
+        sum_out[at] = value
+        within = len(plane)
+
+        @pl.when(odd)
+        def _():
+            for slot, device in enumerate(plane[:-1]):
+                give(at, within + slot, device)
+            rows_moved(at, sum_recv, 2 * within - 1)
+            sum_out[at + 1] = tree([value] + [sum_in[at, slot] for slot in range(2 * within - 1)])
+            for slot, (layer, cell) in enumerate(column):
+                give(at + 1, slot, (layer - 1, cell))
+                give(at + 1, slot, (layer, cell))
+            give(at + 1, len(column), (g - 1, x))
+            rows_moved(at + 1, sum_recv, len(column))
+
+        @pl.when(jnp.logical_not(odd))
+        def _():
+            for slot, device in enumerate(plane):
+                give(at, slot, device)
+            rows_moved(at + 1, sum_recv, len(column) + 1)
+            sum_out[at + 1] = sum_in[at + 1, len(column)]
+
+        return tree([sum_out[at + 1]] + [sum_in[at + 1, slot] for slot in range(len(column))])
 
     pass_token(0)
     factors = momentum_factors(ITERS)
@@ -419,7 +435,7 @@
     guess = [alive * (current[r] + factors[0] * (current[r] - earlier[r])) for r in range(3)]
     for iteration in range(ITERS):
         phase = 3 * iteration
-        velocity = free + weights * collect(phase, guess, set_halo if iteration == 0 else None)
+        velocity = free + weights * collect(phase, guess, *((set_near, set_halo) if iteration == 0 else ()))
         if iteration == 0:
             pl.semaphore_wait(token_sems.at[0], len(tokens[0]))
             pass_token(1)
@@ -456,12 +472,17 @@
 
     for phase in range(PHASES):
         await_segments(phase, phase_send, downward if phase in SPREADS else upward)
-    for at in range(ITERS * ROUNDS):
-        gone = sum_in.at[at, pl.ds(0, len(peers[0]) if at % ROUNDS == 0 else 2 * len(peers[1]))]
-
-        @pl.when(jnp.logical_or(at % ROUNDS == 0, g % 2 == 1))
+    for iteration in range(ITERS):
+        at = iteration * ROUNDS
+
+        @pl.when(odd)
         def _():
-            pltpu.make_async_copy(gone, gone, sum_send.at[at]).wait()
+            rows_moved(at, sum_send, len(plane) - 1)
+            rows_moved(at + 1, sum_send, 2 * len(column) + 1)
+
+        @pl.when(jnp.logical_not(odd))
+        def _():
+            rows_moved(at, sum_send, len(plane))
 
 
 def solution(mesh):

time: 70.2 us -> 69.7 us (level)
  no operation moved by 1% of the time
where the time goes in v4:
time: 69.7 us; the launch traced here: 69.5 us
  Pallas kernels  66.9 us (96%)
  local copies, waits for them, and re-layouts  1.96 us (3%)
    pallas_call x1, Pallas kernels, on_device(): pl.pallas_call(functools.partial(kernel, layers, cells, depth), out_shape...  66.9 us
    unnamed x4, local copies, waits for them, and re-layouts  1.96 us

profile of v4, /device:TPU:1, one launch (start us, length us, event | category | flops | bytes accessed | tf_op | source)
XLA Modules:
  0.0 69.5 jit_solution(6747816558260090696)
XLA Ops:
  0.6 66.9 %shard_map.140 = (f32[3,1,2048]{2,1,0:T(1,128)}, f32[6,1,512]{2,1,0:T(1,128)}) custom-call(f32[6,1,512]{2,1,0:T(1,128)} %bitcast.23, f32[2,512]{1,0:T(2,128)} %bitcast.30, f32[576,128]{1,0:T(8,128)} %bitcast.19, f32[3,1,2048]{2,1,0:T(1,128)} %bitcast.20, f32[3,1,2048]{2,1,0:T(1,128)} %bitcast.21, f32[1,2048]{1,0:T(1,128)} %bitcast.25, f32[1,2048]{1,0:T(1,128)} %bitcast.26, ...), custom_call_target="tpu_custom_call" | custom-call | tf_op jit(solution)/shard_map/pallas_call | solution.py:527
  67.5 0.0 copy-start
  67.5 1.4 %copy.19 = f32[1,1,3,2048]{3,1,2,0:T(1,128)} copy(f32[1,1,3,2048]{3,1,2,0:T(1,128)} %bitcast.22) | data formatting | bytes 49152
  68.9 0.0 copy-done
  68.9 0.6 copy.20
Async XLA Ops:
  67.5 1.4 %copy-start = (f32[6,1,512]{2,1,0:T(1,128)S(1)}, f32[6,1,512]{2,1,0:T(1,128)}, u32[]{:S(2)}) copy-start(f32[6,1,512]{2,1,0:T(1,128)} %get-tuple-element.5) | copy-start | bytes 36868

commit v5 on v4

--- a/solution.py
+++ b/solution.py
@@ -190,7 +190,7 @@
                 (far_hbm, far_ref),
                 (near_hbm, near_ref),
                 (side_hbm, side_ref),
-                (jacobian_hbm, jacobian_ref),
+                (jacobian_hbm, jacobian_ref.at[pl.ds(0, jacobian_hbm.shape[0])]),
                 (impulses_hbm, impulses_ref),
                 (previous_hbm, previous_ref),
                 (counts_hbm, counts_ref),
@@ -553,7 +553,10 @@
                 pltpu.SemaphoreType.DMA((sums,)),
                 pltpu.SemaphoreType.DMA((sums,)),
                 pltpu.SemaphoreType.REGULAR((2,)),
-                *[pltpu.VMEM(v.shape, v.dtype) for v in operands],
+                *[
+                    pltpu.VMEM((v.shape[0] + 4 * contacts // 128, 128), F32) if v is operands[2] else pltpu.VMEM(v.shape, v.dtype)
+                    for v in operands
+                ],
                 pltpu.SemaphoreType.DMA((len(operands),)),
             ],
             compiler_params=pltpu.CompilerParams(

time: 69.7 us -> 69.7 us (level)
  no operation moved by 1% of the time
where the time goes in v5:
time: 69.7 us; the launch traced here: 69.5 us
  Pallas kernels  66.9 us (96%)
  local copies, waits for them, and re-layouts  1.96 us (3%)
    pallas_call x1, Pallas kernels, on_device(): pl.pallas_call(functools.partial(kernel, layers, cells, depth), out_shape...  66.9 us
    unnamed x4, local copies, waits for them, and re-layouts  1.96 us

profile of v5, /device:TPU:1, one launch (start us, length us, event | category | flops | bytes accessed | tf_op | source)
XLA Modules:
  0.0 69.5 jit_solution(9549682765380180573)
XLA Ops:
  0.6 66.9 %shard_map.140 = (f32[3,1,2048]{2,1,0:T(1,128)}, f32[6,1,512]{2,1,0:T(1,128)}) custom-call(f32[6,1,512]{2,1,0:T(1,128)} %bitcast.23, f32[2,512]{1,0:T(2,128)} %bitcast.30, f32[576,128]{1,0:T(8,128)} %bitcast.19, f32[3,1,2048]{2,1,0:T(1,128)} %bitcast.20, f32[3,1,2048]{2,1,0:T(1,128)} %bitcast.21, f32[1,2048]{1,0:T(1,128)} %bitcast.25, f32[1,2048]{1,0:T(1,128)} %bitcast.26, ...), custom_call_target="tpu_custom_call" | custom-call | tf_op jit(solution)/shard_map/pallas_call | solution.py:527
  67.5 0.0 copy-start
  67.5 1.4 %copy.19 = f32[1,1,3,2048]{3,1,2,0:T(1,128)} copy(f32[1,1,3,2048]{3,1,2,0:T(1,128)} %bitcast.22) | data formatting | bytes 49152
  68.9 0.0 copy-done
  68.9 0.6 copy.20
Async XLA Ops:
  67.5 1.4 %copy-start = (f32[6,1,512]{2,1,0:T(1,128)S(1)}, f32[6,1,512]{2,1,0:T(1,128)}, u32[]{:S(2)}) copy-start(f32[6,1,512]{2,1,0:T(1,128)} %get-tuple-element.5) | copy-start | bytes 36868
